TPU v7x, 32 devices: a whole 2x2x4 slice. The times are simulated.
32 devices in a mesh: seg: 4 (over z), mpo: 4 (over x, core), sec: 2 (over y).
Axes of the slice: x: 2, y: 2, z: 4, core: 2. Of those that a mesh axis runs over, the one named last changes fastest.
Arguments:
- state: bfloat16 [4, 1024, 1024], P('seg', 'sec'), may hold values from -6 to 6
- left_env: bfloat16 [4, 12, 1024, 1024], P('seg', 'mpo', 'sec'), may hold values from -0.1875 to 0.1875
- right_env: bfloat16 [4, 12, 1024, 1024], P('seg', 'mpo'), may hold values from -0.1875 to 0.1875
- inv_singular: float32 [4, 1024], P('seg'), may hold values from 0.5 to 2
- sketch_cols: bfloat16 [4, 2, 1024, 256], P('seg'), may hold values from -6 to 6
- kept_ranks: int32 [4], P('seg'), may hold values from 128 to 256, as said below
Outputs:
- final_state: bfloat16 [4, 1024, 1024], P('seg', 'sec')
Inputs may be any that keep to these rules, and one draw needn't show every extreme that they name: `kept_ranks`: each segment keeps between 128 and 256 ranks; some segment keeps exactly 256.
All inputs are finite; a program needn't handle non-finite values.
Results may differ from a plain program's by a relative error of at most 0.025.
Values may be sent and summed in bfloat16 or wider, within the bound.
No kernel may reach another device: no remote copies, remote signals or barrier semaphores. Data moves between devices by JAX's collectives and lax.ppermute only.
A program may use at most 128 MiB of HBM per device.

v0:
```python
import jax
import jax.numpy as jnp
from jax import lax
from jax.sharding import PartitionSpec as P

ITERS = 2
TAU = 0.3
MOMENTUM = 0.5
EPS = 1e-06


def from_behind(block, axis, distance):
    devices = range(lax.axis_size(axis))
    route = [(i - distance, i) for i in devices if i - distance in devices]
    return lax.ppermute(block, axis, route)


def left_products(left, rows):
    return jnp.einsum(
        "kij,jn->kin",
        left,
        lax.all_gather(rows, "sec", axis=0, tiled=True),
        preferred_element_type=jnp.float32,
    )


def gradient_step(rows, previous, left, right):
    width = rows.shape[1]
    first = left_products(left, rows).astype(jnp.bfloat16)
    partial_sum = jnp.einsum("kij,kjn->in", first, right, preferred_element_type=jnp.float32)
    total = lax.psum(partial_sum, "mpo")
    shifted = rows.astype(jnp.float32) - TAU * total
    if previous is not None:
        shifted = shifted - MOMENTUM * previous.astype(jnp.float32)
    squares = lax.psum(jnp.sum(shifted * shifted), "sec")
    return (shifted * (width * lax.rsqrt(squares + EPS))).astype(jnp.bfloat16)


def run_steps(start_rows, left, right):
    current = start_rows
    previous = None
    for step in range(ITERS):
        current, previous = (gradient_step(current, previous, left, right), current)
    return current


def truncate(rows, omega, rank):
    columns = omega.shape[1]
    sketch = jnp.dot(rows, omega, preferred_element_type=jnp.float32)
    keep = (jnp.arange(columns) < rank).astype(jnp.float32)
    as_float = rows.astype(jnp.float32)
    gram, cross = lax.psum(
        (
            jnp.dot(sketch.T, sketch, precision=lax.Precision.HIGHEST),
            jnp.dot(sketch.T, as_float, precision=lax.Precision.HIGHEST),
        ),
        "sec",
    )
    factor = jnp.linalg.cholesky(gram)
    basis = (
        lax.linalg.triangular_solve(factor, sketch.T, left_side=True, lower=True).T * keep[None, :]
    )
    coeffs = lax.linalg.triangular_solve(factor, cross, left_side=True, lower=True) * keep[:, None]
    return jnp.dot(basis, coeffs, precision=lax.Precision.HIGHEST).astype(jnp.bfloat16)


def on_device(state, left_env, right_env, inv_singular, sketch_cols, kept_ranks):
    rows = state[0]
    left = left_env[0]
    right = right_env[0]
    scales = inv_singular[0]
    rank = kept_ranks[0]
    width = rows.shape[1]
    neighbour = from_behind(rows, "seg", 1)
    merged = (rows.astype(jnp.float32) + neighbour.astype(jnp.float32) * scales[None, :]).astype(
        jnp.bfloat16
    )
    current = run_steps(merged, left, right)
    middle = truncate(current, sketch_cols[0, 0], rank)
    expanded = left_products(left, middle).astype(jnp.bfloat16)
    summed = lax.psum_scatter(
        jnp.einsum("ia,kin->akn", middle, expanded, preferred_element_type=jnp.float32),
        "sec",
        scatter_dimension=0,
        tiled=True,
    )
    message = (summed * (1.0 / width)).astype(jnp.bfloat16)
    arrived = from_behind(message, "seg", 1)
    left_next = (
        left.astype(jnp.float32) + jnp.transpose(arrived.astype(jnp.float32), (1, 0, 2))
    ).astype(jnp.bfloat16)
    neighbour_two = from_behind(middle, "seg", -1)
    merged_two = (
        middle.astype(jnp.float32) + neighbour_two.astype(jnp.float32) * scales[None, :]
    ).astype(jnp.bfloat16)
    current = run_steps(merged_two, left_next, right)
    final_rows = truncate(current, sketch_cols[0, 1], rank)
    return final_rows[None]


def solution(mesh):
    return jax.shard_map(
        on_device,
        mesh=mesh,
        in_specs=(
            P("seg", "sec", None),
            P("seg", "mpo", "sec", None),
            P("seg", "mpo", None, None),
            P("seg", None),
            P("seg", None, None, None),
            P("seg"),
        ),
        out_specs=P("seg", "sec", None),
        check_vma=False,
    )
```

profile of v0, /device:TPU:0, one launch (start us, length us, event | category | flops | bytes accessed | tf_op | source)
XLA Modules:
  0.0 956.5 jit_solution(16439634779600430897)
XLA Ops:
  11.5 22.6 %collective-permute-done = bf16[512,1024]{1,0:T(8,128)(2,1)S(1)} collective-permute-done((bf16[512,1024]{1,0:T(8,128)(2,1)}, bf16[512,1024]{1,0:T(8,128)(2,1)S(1)}, u32[]{:S(2)}, u32[]{:S(2)}) %collective-permute-start) | collective-permute-done | bytes 1048608 | tf_op jit(solution)/shard_map/ppermute | solution.py:15
  36.9 35.3 %all-gather.6.cloned.1.call-done = bf16[1024,1024]{1,0:T(8,128)(2,1)} async-done(((bf16[512,1024]{1,0:T(8,128)(2,1)}), bf16[1024,1024]{1,0:T(8,128)(2,1)}) %all-gather.6.cloned.1.call-update) | async-done | bytes 2097168 | tf_op jit(solution)/shard_map/all_gather | solution.py:22
  77.4 7.5 fusion.33
  85.1 51.5 %all-reduce.10.cloned.1.call-done = f32[512,1024]{1,0:T(8,128)} async-done(((f32[512,1024]{1,0:T(8,128)}), f32[512,1024]{1,0:T(8,128)}) %all-reduce.10.cloned.1.call-update) | async-done | bytes 2097168 | tf_op jit(solution)/shard_map/psum | solution.py:31
  139.4 5.5 psum.85
  147.3 33.1 %all-gather.8.cloned.1.call-done = bf16[1024,1024]{1,0:T(8,128)(2,1)} async-done(((bf16[512,1024]{1,0:T(8,128)(2,1)}), bf16[1024,1024]{1,0:T(8,128)(2,1)}) %all-gather.8.cloned.1.call-update) | async-done | bytes 2097168 | tf_op jit(solution)/shard_map/all_gather | solution.py:22
  180.4 5.9 fusion.15
  186.4 7.5 fusion.38
  194.0 51.5 %all-reduce.12.cloned.1.call-done = f32[512,1024]{1,0:T(8,128)} async-done(((f32[512,1024]{1,0:T(8,128)}), f32[512,1024]{1,0:T(8,128)}) %all-reduce.12.cloned.1.call-update) | async-done | bytes 2097168 | tf_op jit(solution)/shard_map/psum | solution.py:31
  261.9 45.3 %all-reduce.20.cloned.1.call-done = (f32[256,1024]{1,0:T(8,128)}, f32[256,256]{0,1:T(8,128)}) async-done(((f32[256,1024]{1,0:T(8,128)}, f32[256,256]{0,1:T(8,128)}), (f32[256,1024]{1,0:T(8,128)}, f32[256,256]{0,1:T(8,128)})) %all-reduce.20.cloned.1.call-update) | async-done | bytes 1310736 | tf_op jit(solution)/shard_map/psum | solution.py:52
  309.2 11.7 %cholesky.130 = f32[128,128]{1,0:T(8,128)S(1)} custom-call(f32[128,128]{1,0:T(8,128)S(1)} %cholesky.194), custom_call_target="Cholesky" | custom-call | tf_op jit(solution)/shard_map/jit(cholesky)/cholesky | solution.py:59
  321.0 9.8 %custom-call.17 = f32[1,128,128]{1,2,0:T(8,128)S(1)} custom-call(f32[1,128,128]{2,1,0:T(8,128)S(1)} %get-tuple-element.71), custom_call_target="InvertDiagBlocksLowerTriangular" | custom-call | tf_op jit(solution)/shard_map/jit(cholesky)/cholesky | solution.py:59
  331.3 11.7 %cholesky.147 = f32[128,128]{1,0:T(8,128)S(1)} custom-call(f32[128,128]{1,0:T(8,128)S(1)} %convolution_subtract_fusion.5), custom_call_target="Cholesky" | custom-call | tf_op jit(solution)/shard_map/jit(cholesky)/cholesky | solution.py:59
  349.8 19.7 %custom-call.18 = f32[2,128,128]{1,2,0:T(8,128)S(1)} custom-call(f32[2,128,128]{2,1,0:T(8,128)S(1)} %get-tuple-element.36), custom_call_target="InvertDiagBlocksLowerTriangular" | custom-call | tf_op jit(solution)/shard_map/triangular_solve/custom-call.0 | solution.py:61
  375.9 33.2 %all-gather.10.cloned.1.call-done = bf16[1024,1024]{1,0:T(8,128)(2,1)} async-done(((bf16[512,1024]{1,0:T(8,128)(2,1)}), bf16[1024,1024]{1,0:T(8,128)(2,1)}) %all-gather.10.cloned.1.call-update) | async-done | bytes 2097168 | tf_op jit(solution)/shard_map/all_gather | solution.py:22
  409.1 11.1 %fusion.9 = f32[1024,3,1024]{2,0,1:T(8,128)} fusion(bf16[1,3,512,1024]{3,2,1,0:T(8,128)(2,1)S(1)} %copy-done.11, bf16[1024,1024]{1,0:T(8,128)(2,1)} %all-gather.10.cloned.1.call-done, bf16[512,1024]{1,0:T(8,128)(2,1)} %convolution_convert_fusion.1), kind=kOutput, calls=%fused_computation.15 | convolution fusion | flops 6444023808 | bytes 18874368 | tf_op jit(solution)/shard_map/ia,kin->akn/dot_general | solution.py:82
  422.7 142.1 %reduce-scatter.2.cloned.1.call-done = f32[512,3,1024]{2,0,1:T(8,128)} async-done(((f32[1024,3,1024]{2,0,1:T(8,128)}), f32[512,3,1024]{2,0,1:T(8,128)}) %reduce-scatter.2.cloned.1.call-update) | async-done | bytes 6291472 | tf_op jit(solution)/shard_map/reduce_scatter | solution.py:81
  576.9 30.5 %all-gather.12.cloned.1.call-done = bf16[1024,1024]{1,0:T(8,128)(2,1)} async-done(((bf16[512,1024]{1,0:T(8,128)(2,1)}), bf16[1024,1024]{1,0:T(8,128)(2,1)}) %all-gather.12.cloned.1.call-update) | async-done | bytes 2097168 | tf_op jit(solution)/shard_map/all_gather | solution.py:22
  607.4 33.9 %collective-permute-done.2 = bf16[512,3,1024]{2,0,1:T(8,128)(2,1)} collective-permute-done((bf16[512,3,1024]{2,0,1:T(8,128)(2,1)}, bf16[512,3,1024]{2,0,1:T(8,128)(2,1)}, u32[]{:S(2)}, u32[]{:S(2)}) %collective-permute-start.2) | collective-permute-done | bytes 3145760 | tf_op jit(solution)/shard_map/ppermute | solution.py:15
  641.3 6.9 fusion.28
  648.2 7.6 fusion.43
  655.9 52.5 %all-reduce.14.cloned.1.call-done = f32[512,1024]{1,0:T(8,128)} async-done(((f32[512,1024]{1,0:T(8,128)}), f32[512,1024]{1,0:T(8,128)}) %all-reduce.14.cloned.1.call-update) | async-done | bytes 2097168 | tf_op jit(solution)/shard_map/psum | solution.py:31
  718.9 33.3 %all-gather.14.cloned.1.call-done = bf16[1024,1024]{1,0:T(8,128)(2,1)} async-done(((bf16[512,1024]{1,0:T(8,128)(2,1)}), bf16[1024,1024]{1,0:T(8,128)(2,1)}) %all-gather.14.cloned.1.call-update) | async-done | bytes 2097168 | tf_op jit(solution)/shard_map/all_gather | solution.py:22
  752.3 6.9 fusion.26
  759.2 7.5 fusion.48
  766.8 51.5 %all-reduce.16.cloned.1.call-done = f32[512,1024]{1,0:T(8,128)} async-done(((f32[512,1024]{1,0:T(8,128)}), f32[512,1024]{1,0:T(8,128)}) %all-reduce.16.cloned.1.call-update) | async-done | bytes 2097168 | tf_op jit(solution)/shard_map/psum | solution.py:31
  821.0 5.8 psum.93
  834.0 46.2 %all-reduce.18.cloned.1.call-done = (f32[256,1024]{1,0:T(8,128)}, f32[256,256]{0,1:T(8,128)}) async-done(((f32[256,1024]{1,0:T(8,128)}, f32[256,256]{0,1:T(8,128)}), (f32[256,1024]{1,0:T(8,128)}, f32[256,256]{0,1:T(8,128)})) %all-reduce.18.cloned.1.call-update) | async-done | bytes 1310736 | tf_op jit(solution)/shard_map/psum | solution.py:52
  882.2 11.7 %cholesky.164 = f32[128,128]{1,0:T(8,128)S(1)} custom-call(f32[128,128]{1,0:T(8,128)S(1)} %cholesky.197), custom_call_target="Cholesky" | custom-call | tf_op jit(solution)/shard_map/jit(cholesky)/cholesky | solution.py:59
  894.0 9.8 %custom-call.20 = f32[1,128,128]{1,2,0:T(8,128)S(1)} custom-call(f32[1,128,128]{2,1,0:T(8,128)S(1)} %get-tuple-element.67), custom_call_target="InvertDiagBlocksLowerTriangular" | custom-call | tf_op jit(solution)/shard_map/jit(cholesky)/cholesky | solution.py:59
  904.3 11.9 %cholesky.181 = f32[128,128]{1,0:T(8,128)S(1)} custom-call(f32[128,128]{1,0:T(8,128)S(1)} %convolution_subtract_fusion.4), custom_call_target="Cholesky" | custom-call | tf_op jit(solution)/shard_map/jit(cholesky)/cholesky | solution.py:59
  923.2 19.7 %custom-call.21 = f32[2,128,128]{1,2,0:T(8,128)S(1)} custom-call(f32[2,128,128]{2,1,0:T(8,128)S(1)} %get-tuple-element.38), custom_call_target="InvertDiagBlocksLowerTriangular" | custom-call | tf_op jit(solution)/shard_map/triangular_solve/custom-call.0 | solution.py:61
  (130 shorter events, 103.1 us)
Async XLA Ops:
  6.5 65.7 %all-gather.6.cloned.1.call-start = ((), (), s32[]{:S(2)}) async-start(), calls=%async_computation.1 | async-start | bytes 3145728 | tf_op jit(solution)/shard_map/all_gather | solution.py:22
  6.5 27.6 %collective-permute-start = (bf16[512,1024]{1,0:T(8,128)(2,1)}, bf16[512,1024]{1,0:T(8,128)(2,1)S(1)}, u32[]{:S(2)}, u32[]{:S(2)}) collective-permute-start(bf16[512,1024]{1,0:T(8,128)(2,1)} %bitcast.191), channel_id=1, source_target_pairs={{0,8},{8,16},{16,24},{1,9},{9,17},{17,25},{2,10},{10,18},{18,26},{... | collective-permute-start | bytes 3145736 | tf_op jit(solution)/shard_map/ppermute | solution.py:15
  34.2 38.0 %copy-start.10 = (bf16[1,3,512,1024]{3,2,1,0:T(8,128)(2,1)S(1)}, bf16[1,3,512,1024]{3,2,1,0:T(8,128)(2,1)}, u32[]{:S(2)}) copy-start(bf16[1,3,512,1024]{3,2,1,0:T(8,128)(2,1)} %param.12) | copy-start | bytes 9437188
  36.9 99.6 %all-reduce.10.cloned.1.call-start = ((), (), s32[]{:S(2)}) async-start(), calls=%async_computation.2 | async-start | bytes 4194304 | tf_op jit(solution)/shard_map/psum | solution.py:31
  85.0 51.6 %copy-start.1 = (bf16[512,1024]{1,0:T(8,128)(2,1)S(1)}, bf16[512,1024]{1,0:T(8,128)(2,1)}, u32[]{:S(2)}) copy-start(bf16[512,1024]{1,0:T(8,128)(2,1)} %add_convert_fusion.1) | copy-start | bytes 3145732
  85.0 95.4 %all-gather.8.cloned.1.call-start = ((), (), s32[]{:S(2)}) async-start(), calls=%async_computation.3 | async-start | bytes 3145728 | tf_op jit(solution)/shard_map/all_gather | solution.py:22
  136.5 9.1 copy-start.5
  147.1 98.4 %all-reduce.12.cloned.1.call-start = ((), (), s32[]{:S(2)}) async-start(), calls=%async_computation.4 | async-start | bytes 4194304 | tf_op jit(solution)/shard_map/psum | solution.py:31
  193.9 51.6 %copy-start.3 = (bf16[512,1024]{1,0:T(8,128)(2,1)S(1)}, bf16[512,1024]{1,0:T(8,128)(2,1)}, u32[]{:S(2)}) copy-start(bf16[512,1024]{1,0:T(8,128)(2,1)} %multiply_convert_fusion.4) | copy-start | bytes 3145732
  193.9 113.2 %all-reduce.20.cloned.1.call-start = ((), (), s32[]{:S(2)}) async-start(), calls=%async_computation.12 | async-start | bytes 2621440 | tf_op jit(solution)/shard_map/psum | solution.py:52
  254.5 2.3 copy-start.12
  261.0 148.1 %all-gather.10.cloned.1.call-start = ((), (), s32[]{:S(2)}) async-start(), calls=%async_computation.5 | async-start | bytes 3145728 | tf_op jit(solution)/shard_map/all_gather | solution.py:22
  330.8 40.1 %copy-start.7 = (f32[256,1024]{1,0:T(8,128)S(1)}, f32[256,1024]{1,0:T(8,128)}, u32[]{:S(2)}) copy-start(f32[256,1024]{1,0:T(8,128)} %get-tuple-element.58) | copy-start | bytes 3145732
  372.8 36.3 %copy-start.11 = (bf16[1,3,512,1024]{3,2,1,0:T(8,128)(2,1)S(1)}, bf16[1,3,512,1024]{3,2,1,0:T(8,128)(2,1)}, u32[]{:S(2)}) copy-start(bf16[1,3,512,1024]{3,2,1,0:T(8,128)(2,1)} %param.12) | copy-start | bytes 9437188
  375.8 189.0 %reduce-scatter.2.cloned.1.call-start = ((), (), s32[]{:S(2)}) async-start(), calls=%async_computation.6 | async-start | bytes 18874368 | tf_op jit(solution)/shard_map/reduce_scatter | solution.py:81
  420.2 1.2 copy-start.4
  420.2 155.1 %copy-start.9 = (f32[1,1024]{1,0:T(1,128)S(1)}, f32[1,1024]{1,0:T(1,128)}, u32[]{:S(2)}) copy-start(f32[1,1024]{1,0:T(1,128)} %param.14) | copy-start | bytes 12292
  420.2 187.2 %all-gather.12.cloned.1.call-start = ((), (), s32[]{:S(2)}) async-start(), calls=%async_computation.7 | async-start | bytes 3145728 | tf_op jit(solution)/shard_map/all_gather | solution.py:22
  421.4 153.9 %collective-permute-start.1 = (bf16[512,1024]{1,0:T(8,128)(2,1)S(1)}, bf16[512,1024]{1,0:T(8,128)(2,1)S(1)}, u32[]{:S(2)}, u32[]{:S(2)}) collective-permute-start(bf16[512,1024]{1,0:T(8,128)(2,1)S(1)} %copy-done.4), channel_id=1, source_target_pairs={{8,0},{16,8},{24,16},{9,1},{17,9},{25,17},{10,2},{18,10},{26,18},{... | collective-permute-start | bytes 3145736 | tf_op jit(solution)/shard_map/ppermute | solution.py:15
  570.2 71.0 %collective-permute-start.2 = (bf16[512,3,1024]{2,0,1:T(8,128)(2,1)}, bf16[512,3,1024]{2,0,1:T(8,128)(2,1)}, u32[]{:S(2)}, u32[]{:S(2)}) collective-permute-start(bf16[512,3,1024]{2,0,1:T(8,128)(2,1)} %multiply_convert_fusion), channel_id=1, source_target_pairs={{0,8},{8,16},{16,24},{1,9},{9,17},{17,25},{2,10},{10,18},{18,26},{... | collective-permute-start | bytes 9437192 | tf_op jit(solution)/shard_map/ppermute | solution.py:15
  576.7 131.7 %all-reduce.14.cloned.1.call-start = ((), (), s32[]{:S(2)}) async-start(), calls=%async_computation.8 | async-start | bytes 4194304 | tf_op jit(solution)/shard_map/psum | solution.py:31
  655.8 52.6 %copy-start = (bf16[512,1024]{1,0:T(8,128)(2,1)S(1)}, bf16[512,1024]{1,0:T(8,128)(2,1)}, u32[]{:S(2)}) copy-start(bf16[512,1024]{1,0:T(8,128)(2,1)} %add_convert_fusion) | copy-start | bytes 3145732
  655.8 96.4 %all-gather.14.cloned.1.call-start = ((), (), s32[]{:S(2)}) async-start(), calls=%async_computation.9 | async-start | bytes 3145728 | tf_op jit(solution)/shard_map/all_gather | solution.py:22
  708.4 9.1 copy-start.6
  718.9 99.4 %all-reduce.16.cloned.1.call-start = ((), (), s32[]{:S(2)}) async-start(), calls=%async_computation.10 | async-start | bytes 4194304 | tf_op jit(solution)/shard_map/psum | solution.py:31
  766.7 51.6 %copy-start.2 = (bf16[512,1024]{1,0:T(8,128)(2,1)S(1)}, bf16[512,1024]{1,0:T(8,128)(2,1)}, u32[]{:S(2)}) copy-start(bf16[512,1024]{1,0:T(8,128)(2,1)} %multiply_convert_fusion.2) | copy-start | bytes 3145732
  766.7 113.4 %all-reduce.18.cloned.1.call-start = ((), (), s32[]{:S(2)}) async-start(), calls=%async_computation.11 | async-start | bytes 2621440 | tf_op jit(solution)/shard_map/psum | solution.py:52
  827.5 2.3 copy-start.13
  903.8 40.5 %copy-start.8 = (f32[256,1024]{1,0:T(8,128)S(1)}, f32[256,1024]{1,0:T(8,128)}, u32[]{:S(2)}) copy-start(f32[256,1024]{1,0:T(8,128)} %get-tuple-element.56) | copy-start | bytes 3145732
Sparse Core Ops, SparseCore 0:
  37.0 35.1 all-gather.5
  85.1 51.3 all-reduce.9
  147.2 33.1 all-gather.7
  194.0 51.3 all-reduce.11
  261.1 46.0 all-reduce.19
  375.9 33.0 all-gather.9
  420.3 144.4 reduce-scatter.1
  576.8 30.5 all-gather.11
  655.9 52.3 all-reduce.13
  719.0 33.1 all-gather.13
  766.8 51.3 all-reduce.15
  834.1 46.0 all-reduce.17
where the time goes:
time: 962 us; the launch traced here: 956 us
  waiting for transfers between devices  663 us (69%)
  other arithmetic  138 us (14%)
  matrix products  88.1 us (9%)
  blocking collectives  22.4 us (2%)
  between operations  20.6 us (2%)
  starting transfers between devices  12.3 us (1%)
  local copies, waits for them, and re-layouts  11.6 us (1%)
    psum x4, waiting for transfers between devices, gradient_step(): total = lax.psum(partial_sum, 'mpo')  207 us
    all_gather x5, waiting for transfers between devices, left_products(): lax.all_gather(rows, 'sec', axis=0, tiled=True)  165 us
    reduce_scatter x1, waiting for transfers between devices, on_device(): lax.psum_scatter(jnp.einsum('ia,kin->akn', middle, expanded, preferred_el...  142 us
    psum x2, waiting for transfers between devices, truncate(): lax.psum((jnp.dot(sketch.T, sketch, precision=lax.Precision.HIGHEST), jnp...  91.4 us
    another operation x13, other arithmetic, truncate(): factor = jnp.linalg.cholesky(gram)  68.9 us
    ppermute x3, waiting for transfers between devices, from_behind(): return lax.ppermute(block, axis, route)  56.5 us
    another operation x5, other arithmetic, truncate(): lax.linalg.triangular_solve(factor, sketch.T, left_side=True, lower=True)  39.4 us
    dot_general x4, matrix products, gradient_step(): jnp.einsum('kij,kjn->in', first, right, preferred_element_type=jnp.float32)  30.2 us
  transfers between devices with their start and end apart: 15, of which 14 were waited for; matrix products, arithmetic and copies ran while one was open for 1% of the time, Pallas kernels for 0%

commit v1 on v0

--- a/solution.py
+++ b/solution.py
@@ -28,7 +28,7 @@
     width = rows.shape[1]
     first = left_products(left, rows).astype(jnp.bfloat16)
     partial_sum = jnp.einsum("kij,kjn->in", first, right, preferred_element_type=jnp.float32)
-    total = lax.psum(partial_sum, "mpo")
+    total = jnp.sum(lax.all_gather(partial_sum, "mpo"), axis=0)
     shifted = rows.astype(jnp.float32) - TAU * total
     if previous is not None:
         shifted = shifted - MOMENTUM * previous.astype(jnp.float32)

time: 962 us -> 1000 us (1.040)
  waiting for transfers between devices: 663 us -> 690 us
  other arithmetic: 138 us -> 152 us
    all_gather x0 -> x4, waiting for transfers between devices: none -> 235 us  [gradient_step(): total = jnp.sum(lax.all_gather(partial_sum, 'mpo'), axis=0)]
    psum x4 -> x0, waiting for transfers between devices: 207 us -> none  [gradient_step(): total = lax.psum(partial_sum, 'mpo')]
    reduce_sum x0 -> x4, other arithmetic: none -> 18.4 us  [gradient_step(): total = jnp.sum(lax.all_gather(partial_sum, 'mpo'), axis=0)]
where the time goes in v1:
time: 1000 us; the launch traced here: 998 us
  waiting for transfers between devices  690 us (69%)
  other arithmetic  152 us (15%)
  matrix products  88.4 us (9%)
  blocking collectives  22.6 us (2%)
  between operations  20.7 us (2%)
  starting transfers between devices  12.4 us (1%)
  local copies, waits for them, and re-layouts  11.6 us (1%)
    all_gather x4, waiting for transfers between devices, gradient_step(): total = jnp.sum(lax.all_gather(partial_sum, 'mpo'), axis=0)  235 us
    all_gather x5, waiting for transfers between devices, left_products(): lax.all_gather(rows, 'sec', axis=0, tiled=True)  165 us
    reduce_scatter x1, waiting for transfers between devices, on_device(): lax.psum_scatter(jnp.einsum('ia,kin->akn', middle, expanded, preferred_el...  142 us
    psum x2, waiting for transfers between devices, truncate(): lax.psum((jnp.dot(sketch.T, sketch, precision=lax.Precision.HIGHEST), jnp...  91.3 us
    another operation x13, other arithmetic, truncate(): factor = jnp.linalg.cholesky(gram)  68.9 us
    ppermute x3, waiting for transfers between devices, from_behind(): return lax.ppermute(block, axis, route)  56.5 us
    another operation x5, other arithmetic, truncate(): lax.linalg.triangular_solve(factor, sketch.T, left_side=True, lower=True)  39.4 us
    dot_general x4, matrix products, gradient_step(): jnp.einsum('kij,kjn->in', first, right, preferred_element_type=jnp.float32)  30.6 us
  transfers between devices with their start and end apart: 15, of which 14 were waited for; matrix products, arithmetic and copies ran while one was open for 1% of the time, Pallas kernels for 0%

profile of v1, /device:TPU:0, one launch (start us, length us, event | category | flops | bytes accessed | tf_op | source)
XLA Modules:
  0.0 998.0 jit_solution(5652541454124897087)
XLA Ops:
  11.5 22.6 %collective-permute-done = bf16[512,1024]{1,0:T(8,128)(2,1)S(1)} collective-permute-done((bf16[512,1024]{1,0:T(8,128)(2,1)}, bf16[512,1024]{1,0:T(8,128)(2,1)S(1)}, u32[]{:S(2)}, u32[]{:S(2)}) %collective-permute-start) | collective-permute-done | bytes 1048608 | tf_op jit(solution)/shard_map/ppermute | solution.py:15
  36.9 35.3 %all-gather.14.cloned.1.call-done = bf16[1024,1024]{1,0:T(8,128)(2,1)} async-done(((bf16[512,1024]{1,0:T(8,128)(2,1)}), bf16[1024,1024]{1,0:T(8,128)(2,1)}) %all-gather.14.cloned.1.call-update) | async-done | bytes 2097168 | tf_op jit(solution)/shard_map/all_gather | solution.py:22
  77.4 7.6 fusion.33
  85.1 58.4 %all-gather.24.cloned.1.call-done = f32[2048,1024]{1,0:T(8,128)} async-done(((f32[512,1024]{1,0:T(8,128)}), f32[2048,1024]{1,0:T(8,128)}) %all-gather.24.cloned.1.call-update) | async-done | bytes 8388624 | tf_op jit(solution)/shard_map/all_gather | solution.py:31
  157.2 33.1 %all-gather.16.cloned.1.call-done = bf16[1024,1024]{1,0:T(8,128)(2,1)} async-done(((bf16[512,1024]{1,0:T(8,128)(2,1)}), bf16[1024,1024]{1,0:T(8,128)(2,1)}) %all-gather.16.cloned.1.call-update) | async-done | bytes 2097168 | tf_op jit(solution)/shard_map/all_gather | solution.py:22
  190.3 5.9 fusion.15
  196.2 7.6 fusion.38
  203.9 58.4 %all-gather.26.cloned.1.call-done = f32[2048,1024]{1,0:T(8,128)} async-done(((f32[512,1024]{1,0:T(8,128)}), f32[2048,1024]{1,0:T(8,128)}) %all-gather.26.cloned.1.call-update) | async-done | bytes 8388624 | tf_op jit(solution)/shard_map/all_gather | solution.py:31
  269.3 5.6 psum.57
  282.8 45.2 %all-reduce.8.cloned.1.call-done = (f32[256,1024]{1,0:T(8,128)}, f32[256,256]{0,1:T(8,128)}) async-done(((f32[256,1024]{1,0:T(8,128)}, f32[256,256]{0,1:T(8,128)}), (f32[256,1024]{1,0:T(8,128)}, f32[256,256]{0,1:T(8,128)})) %all-reduce.8.cloned.1.call-update) | async-done | bytes 1310736 | tf_op jit(solution)/shard_map/psum | solution.py:52
  330.0 11.7 %cholesky.130 = f32[128,128]{1,0:T(8,128)S(1)} custom-call(f32[128,128]{1,0:T(8,128)S(1)} %cholesky.194), custom_call_target="Cholesky" | custom-call | tf_op jit(solution)/shard_map/jit(cholesky)/cholesky | solution.py:59
  341.8 9.8 custom-call.17
  352.1 11.7 %cholesky.147 = f32[128,128]{1,0:T(8,128)S(1)} custom-call(f32[128,128]{1,0:T(8,128)S(1)} %convolution_subtract_fusion.5), custom_call_target="Cholesky" | custom-call | tf_op jit(solution)/shard_map/jit(cholesky)/cholesky | solution.py:59
  370.6 19.7 %custom-call.18 = f32[2,128,128]{1,2,0:T(8,128)S(1)} custom-call(f32[2,128,128]{2,1,0:T(8,128)S(1)} %get-tuple-element.36), custom_call_target="InvertDiagBlocksLowerTriangular" | custom-call | tf_op jit(solution)/shard_map/triangular_solve/custom-call.0 | solution.py:61
  396.7 33.2 %all-gather.18.cloned.1.call-done = bf16[1024,1024]{1,0:T(8,128)(2,1)} async-done(((bf16[512,1024]{1,0:T(8,128)(2,1)}), bf16[1024,1024]{1,0:T(8,128)(2,1)}) %all-gather.18.cloned.1.call-update) | async-done | bytes 2097168 | tf_op jit(solution)/shard_map/all_gather | solution.py:22
  429.9 11.1 %fusion.9 = f32[1024,3,1024]{2,0,1:T(8,128)} fusion(bf16[1,3,512,1024]{3,2,1,0:T(8,128)(2,1)S(1)} %copy-done.7, bf16[1024,1024]{1,0:T(8,128)(2,1)} %all-gather.18.cloned.1.call-done, bf16[512,1024]{1,0:T(8,128)(2,1)} %convolution_convert_fusion.1), kind=kOutput, calls=%fused_computation.15 | convolution fusion | flops 6444023808 | bytes 18874368 | tf_op jit(solution)/shard_map/ia,kin->akn/dot_general | solution.py:82
  443.6 142.1 %reduce-scatter.2.cloned.1.call-done = f32[512,3,1024]{2,0,1:T(8,128)} async-done(((f32[1024,3,1024]{2,0,1:T(8,128)}), f32[512,3,1024]{2,0,1:T(8,128)}) %reduce-scatter.2.cloned.1.call-update) | async-done | bytes 6291472 | tf_op jit(solution)/shard_map/reduce_scatter | solution.py:81
  597.8 30.4 %all-gather.20.cloned.1.call-done = bf16[1024,1024]{1,0:T(8,128)(2,1)} async-done(((bf16[512,1024]{1,0:T(8,128)(2,1)}), bf16[1024,1024]{1,0:T(8,128)(2,1)}) %all-gather.20.cloned.1.call-update) | async-done | bytes 2097168 | tf_op jit(solution)/shard_map/all_gather | solution.py:22
  628.2 33.9 %collective-permute-done.2 = bf16[512,3,1024]{2,0,1:T(8,128)(2,1)} collective-permute-done((bf16[512,3,1024]{2,0,1:T(8,128)(2,1)}, bf16[512,3,1024]{2,0,1:T(8,128)(2,1)}, u32[]{:S(2)}, u32[]{:S(2)}) %collective-permute-start.2) | collective-permute-done | bytes 3145760 | tf_op jit(solution)/shard_map/ppermute | solution.py:15
  662.1 6.9 fusion.28
  669.0 7.7 fusion.43
  676.7 59.4 %all-gather.28.cloned.1.call-done = f32[2048,1024]{1,0:T(8,128)} async-done(((f32[512,1024]{1,0:T(8,128)}), f32[2048,1024]{1,0:T(8,128)}) %all-gather.28.cloned.1.call-update) | async-done | bytes 8388624 | tf_op jit(solution)/shard_map/all_gather | solution.py:31
  749.6 33.2 %all-gather.22.cloned.1.call-done = bf16[1024,1024]{1,0:T(8,128)(2,1)} async-done(((bf16[512,1024]{1,0:T(8,128)(2,1)}), bf16[1024,1024]{1,0:T(8,128)(2,1)}) %all-gather.22.cloned.1.call-update) | async-done | bytes 2097168 | tf_op jit(solution)/shard_map/all_gather | solution.py:22
  782.9 6.9 fusion.26
  789.8 7.6 fusion.48
  797.5 58.4 %all-gather.30.cloned.1.call-done = f32[2048,1024]{1,0:T(8,128)} async-done(((f32[512,1024]{1,0:T(8,128)}), f32[2048,1024]{1,0:T(8,128)}) %all-gather.30.cloned.1.call-update) | async-done | bytes 8388624 | tf_op jit(solution)/shard_map/all_gather | solution.py:31
  862.9 5.8 psum.61
  875.6 46.1 %all-reduce.6.cloned.1.call-done = (f32[256,1024]{1,0:T(8,128)}, f32[256,256]{0,1:T(8,128)}) async-done(((f32[256,1024]{1,0:T(8,128)}, f32[256,256]{0,1:T(8,128)}), (f32[256,1024]{1,0:T(8,128)}, f32[256,256]{0,1:T(8,128)})) %all-reduce.6.cloned.1.call-update) | async-done | bytes 1310736 | tf_op jit(solution)/shard_map/psum | solution.py:52
  923.8 11.7 %cholesky.164 = f32[128,128]{1,0:T(8,128)S(1)} custom-call(f32[128,128]{1,0:T(8,128)S(1)} %cholesky.197), custom_call_target="Cholesky" | custom-call | tf_op jit(solution)/shard_map/jit(cholesky)/cholesky | solution.py:59
  935.5 9.8 custom-call.20
  945.8 11.9 %cholesky.181 = f32[128,128]{1,0:T(8,128)S(1)} custom-call(f32[128,128]{1,0:T(8,128)S(1)} %convolution_subtract_fusion.4), custom_call_target="Cholesky" | custom-call | tf_op jit(solution)/shard_map/jit(cholesky)/cholesky | solution.py:59
  964.7 19.7 %custom-call.21 = f32[2,128,128]{1,2,0:T(8,128)S(1)} custom-call(f32[2,128,128]{2,1,0:T(8,128)S(1)} %get-tuple-element.38), custom_call_target="InvertDiagBlocksLowerTriangular" | custom-call | tf_op jit(solution)/shard_map/triangular_solve/custom-call.0 | solution.py:61
  (126 shorter events, 116.8 us)
Async XLA Ops:
  6.5 65.7 %all-gather.14.cloned.1.call-start = ((), (), s32[]{:S(2)}) async-start(), calls=%async_computation.1 | async-start | bytes 3145728 | tf_op jit(solution)/shard_map/all_gather | solution.py:22
  6.5 27.6 %collective-permute-start = (bf16[512,1024]{1,0:T(8,128)(2,1)}, bf16[512,1024]{1,0:T(8,128)(2,1)S(1)}, u32[]{:S(2)}, u32[]{:S(2)}) collective-permute-start(bf16[512,1024]{1,0:T(8,128)(2,1)} %bitcast.199), channel_id=1, source_target_pairs={{0,8},{8,16},{16,24},{1,9},{9,17},{17,25},{2,10},{10,18},{18,26},{... | collective-permute-start | bytes 3145736 | tf_op jit(solution)/shard_map/ppermute | solution.py:15
  34.2 38.0 %copy-start.6 = (bf16[1,3,512,1024]{3,2,1,0:T(8,128)(2,1)S(1)}, bf16[1,3,512,1024]{3,2,1,0:T(8,128)(2,1)}, u32[]{:S(2)}) copy-start(bf16[1,3,512,1024]{3,2,1,0:T(8,128)(2,1)} %param.12) | copy-start | bytes 9437188
  36.9 106.6 %all-gather.24.cloned.1.call-start = ((), (), s32[]{:S(2)}) async-start(), calls=%async_computation.7 | async-start | bytes 10485760 | tf_op jit(solution)/shard_map/all_gather | solution.py:31
  85.1 105.2 %all-gather.16.cloned.1.call-start = ((), (), s32[]{:S(2)}) async-start(), calls=%async_computation.2 | async-start | bytes 3145728 | tf_op jit(solution)/shard_map/all_gather | solution.py:22
  143.5 4.6 copy-start.1
  157.0 105.3 %all-gather.26.cloned.1.call-start = ((), (), s32[]{:S(2)}) async-start(), calls=%async_computation.8 | async-start | bytes 10485760 | tf_op jit(solution)/shard_map/all_gather | solution.py:31
  203.9 124.1 %all-reduce.8.cloned.1.call-start = ((), (), s32[]{:S(2)}) async-start(), calls=%async_computation.12 | async-start | bytes 2621440 | tf_op jit(solution)/shard_map/psum | solution.py:52
  275.7 1.9 copy-start.8
  281.8 148.1 %all-gather.18.cloned.1.call-start = ((), (), s32[]{:S(2)}) async-start(), calls=%async_computation.3 | async-start | bytes 3145728 | tf_op jit(solution)/shard_map/all_gather | solution.py:22
  351.6 40.1 %copy-start.3 = (f32[256,1024]{1,0:T(8,128)S(1)}, f32[256,1024]{1,0:T(8,128)}, u32[]{:S(2)}) copy-start(f32[256,1024]{1,0:T(8,128)} %get-tuple-element.58) | copy-start | bytes 3145732
  393.6 36.3 %copy-start.7 = (bf16[1,3,512,1024]{3,2,1,0:T(8,128)(2,1)S(1)}, bf16[1,3,512,1024]{3,2,1,0:T(8,128)(2,1)}, u32[]{:S(2)}) copy-start(bf16[1,3,512,1024]{3,2,1,0:T(8,128)(2,1)} %param.12) | copy-start | bytes 9437188
  396.7 189.0 %reduce-scatter.2.cloned.1.call-start = ((), (), s32[]{:S(2)}) async-start(), calls=%async_computation.4 | async-start | bytes 18874368 | tf_op jit(solution)/shard_map/reduce_scatter | solution.py:81
  441.0 1.2 copy-start.2
  441.1 155.1 %copy-start.5 = (f32[1,1024]{1,0:T(1,128)S(1)}, f32[1,1024]{1,0:T(1,128)}, u32[]{:S(2)}) copy-start(f32[1,1024]{1,0:T(1,128)} %param.14) | copy-start | bytes 12292
  441.1 187.1 %all-gather.20.cloned.1.call-start = ((), (), s32[]{:S(2)}) async-start(), calls=%async_computation.5 | async-start | bytes 3145728 | tf_op jit(solution)/shard_map/all_gather | solution.py:22
  442.3 153.9 %collective-permute-start.1 = (bf16[512,1024]{1,0:T(8,128)(2,1)S(1)}, bf16[512,1024]{1,0:T(8,128)(2,1)S(1)}, u32[]{:S(2)}, u32[]{:S(2)}) collective-permute-start(bf16[512,1024]{1,0:T(8,128)(2,1)S(1)} %copy-done.2), channel_id=1, source_target_pairs={{8,0},{16,8},{24,16},{9,1},{17,9},{25,17},{10,2},{18,10},{26,18},{... | collective-permute-start | bytes 3145736 | tf_op jit(solution)/shard_map/ppermute | solution.py:15
  591.1 71.0 %collective-permute-start.2 = (bf16[512,3,1024]{2,0,1:T(8,128)(2,1)}, bf16[512,3,1024]{2,0,1:T(8,128)(2,1)}, u32[]{:S(2)}, u32[]{:S(2)}) collective-permute-start(bf16[512,3,1024]{2,0,1:T(8,128)(2,1)} %multiply_convert_fusion), channel_id=1, source_target_pairs={{0,8},{8,16},{16,24},{1,9},{9,17},{17,25},{2,10},{10,18},{18,26},{... | collective-permute-start | bytes 9437192 | tf_op jit(solution)/shard_map/ppermute | solution.py:15
  597.6 138.5 %all-gather.28.cloned.1.call-start = ((), (), s32[]{:S(2)}) async-start(), calls=%async_computation.9 | async-start | bytes 10485760 | tf_op jit(solution)/shard_map/all_gather | solution.py:31
  676.7 106.2 %all-gather.22.cloned.1.call-start = ((), (), s32[]{:S(2)}) async-start(), calls=%async_computation.6 | async-start | bytes 3145728 | tf_op jit(solution)/shard_map/all_gather | solution.py:22
  736.1 4.6 copy-start
  749.6 106.3 %all-gather.30.cloned.1.call-start = ((), (), s32[]{:S(2)}) async-start(), calls=%async_computation.10 | async-start | bytes 10485760 | tf_op jit(solution)/shard_map/all_gather | solution.py:31
  797.4 124.3 %all-reduce.6.cloned.1.call-start = ((), (), s32[]{:S(2)}) async-start(), calls=%async_computation.11 | async-start | bytes 2621440 | tf_op jit(solution)/shard_map/psum | solution.py:52
  869.5 1.9 copy-start.9
  945.4 40.5 %copy-start.4 = (f32[256,1024]{1,0:T(8,128)S(1)}, f32[256,1024]{1,0:T(8,128)}, u32[]{:S(2)}) copy-start(f32[256,1024]{1,0:T(8,128)} %get-tuple-element.56) | copy-start | bytes 3145732
Sparse Core Ops, SparseCore 0:
  37.0 35.1 all-gather.13
  85.2 58.2 all-gather.23
  157.1 33.1 all-gather.15
  204.0 58.2 all-gather.25
  281.9 45.9 all-reduce.7
  396.8 33.0 all-gather.17
  441.2 144.4 reduce-scatter.1
  597.7 30.4 all-gather.19
  676.8 59.2 all-gather.27
  749.7 33.1 all-gather.21
  797.5 58.2 all-gather.29
  875.7 45.9 all-reduce.5
